TPU v7x, 256 devices: a whole 4x4x8 slice. The times are simulated.
256 devices in a mesh: row: 32 (over y, x, core), col: 8 (over z).
Axes of the slice: x: 4, y: 4, z: 8, core: 2. Of those that a mesh axis runs over, the one named last changes fastest.
Arguments:
- inputs: bfloat16 [768, 12288], P(None, 'col'), may hold values from -6 to 6
- out_grad: bfloat16 [768, 12288], P(None, 'col'), may hold values from -6 to 6
- pre_act: bfloat16 [768, 24576], P('col', 'row'), may hold values from -8 to 8
- w_in: bfloat16 [12288, 24576], P('col', 'row'), may hold values from -0.0546875 to 0.0546875
- w_out: bfloat16 [24576, 12288], P('row', 'col'), may hold values from -0.0390625 to 0.0390625
Outputs:
- grad_inputs: bfloat16 [768, 12288], P('row', 'col')
- grad_w_in: bfloat16 [12288, 24576], P('col', 'row')
- grad_w_out: bfloat16 [24576, 12288], P('row', 'col')
All inputs are finite; a program needn't handle non-finite values.
Results may differ from a plain program's by a relative error of at most 0.0049.
Values may be sent and summed in bfloat16 or wider, within the bound.
A program may use at most 64 MiB of HBM per device.

v0:
```python
import math

import jax
import jax.numpy as jnp
from jax import lax
from jax.sharding import PartitionSpec as P

coef_c = math.sqrt(2.0 / math.pi)


def gelu_parts(pre_values):
    hval = pre_values.astype(jnp.float32)
    tval = jnp.tanh(coef_c * (hval + 0.044715 * hval * hval * hval))
    activ = 0.5 * hval * (1.0 + tval)
    deriv = 0.5 * (1.0 + tval) + 0.5 * hval * (1.0 - tval * tval) * coef_c * (
        1.0 + 3.0 * 0.044715 * hval * hval
    )
    return (activ, deriv)


def per_device(inputs, out_grad, pre_act, w_in, w_out):
    total_tokens = inputs.shape[0]
    scale_value = 1.0 / math.sqrt(total_tokens)
    block = out_grad
    act_share = lax.psum_scatter(
        lax.dot_general(block, w_out, (((1,), (1,)), ((), ())), preferred_element_type=jnp.float32),
        "col",
        scatter_dimension=0,
        tiled=True,
    )
    local_act, local_deriv = gelu_parts(pre_act)
    hid_share = (act_share * local_deriv).astype(jnp.bfloat16)
    activ_all, hid_all = (
        lax.all_gather(local_act.astype(jnp.bfloat16), "col", axis=0, tiled=True),
        lax.all_gather(hid_share, "col", axis=0, tiled=True),
    )
    grad_w_out = lax.dot_general(
        activ_all, out_grad, (((0,), (0,)), ((), ())), preferred_element_type=jnp.float32
    )
    grad_w_out = (grad_w_out * scale_value).astype(jnp.bfloat16)
    grad_w_in = lax.dot_general(
        inputs, hid_all, (((0,), (0,)), ((), ())), preferred_element_type=jnp.float32
    )
    grad_w_in = (grad_w_in * scale_value).astype(jnp.bfloat16)
    block = hid_all
    grad_inputs = lax.psum_scatter(
        lax.dot_general(block, w_in, (((1,), (1,)), ((), ())), preferred_element_type=jnp.float32),
        "row",
        scatter_dimension=0,
        tiled=True,
    )
    return (grad_inputs.astype(jnp.bfloat16), grad_w_in, grad_w_out)


def solution(mesh):
    placed = (P(None, "col"), P(None, "col"), P("col", "row"), P("col", "row"), P("row", "col"))
    return jax.shard_map(
        per_device,
        mesh=mesh,
        in_specs=placed,
        out_specs=(P("row", "col"), P("col", "row"), P("row", "col")),
        check_vma=False,
    )
```

profile of v0, /device:TPU:1, one launch (start us, length us, event | category | flops | bytes accessed | tf_op | source)
XLA Modules:
  0.0 240.8 jit_solution(5547403851123938522)
XLA Ops:
  7.2 0.0 copy-start
  7.2 0.0 reduce-scatter.3.cloned.1.call-start
  7.2 1.6 copy-done
  8.8 5.1 %fusion.12 = f32[768,768]{1,0:T(8,128)} fusion(bf16[768,1536]{1,0:T(8,128)(2,1)S(1)} %copy-done, bf16[768,1536]{1,0:T(8,128)(2,1)} %param.9), kind=kOutput, calls=%fused_computation.21 | convolution fusion | flops 1811939328 | bytes 7077888 | tf_op jit(solution)/shard_map/dot_general | solution.py:26
  13.9 0.0 copy-start.1
  13.9 0.0 reduce-scatter.3.cloned.1.call-update
  14.0 0.0 all-gather.3.cloned.1.call-start
  14.0 43.0 %reduce-scatter.3.cloned.1.call-done = f32[96,768]{1,0:T(8,128)} async-done(((f32[768,768]{1,0:T(8,128)}), f32[96,768]{1,0:T(8,128)}) %reduce-scatter.3.cloned.1.call-update) | async-done | bytes 294928 | tf_op jit(solution)/shard_map/reduce_scatter | solution.py:25
  57.1 0.0 copy-done.1
  57.1 1.9 fusion.8
  58.9 0.0 all-gather.3.cloned.1.call-update
  59.0 0.0 all-gather.5.cloned.1.call-start
  59.0 0.7 all-gather.5.cloned.1.call-update
  59.7 0.0 reduce-scatter.5.cloned.1.call-start
  59.8 36.7 %all-gather.3.cloned.1.call-done = bf16[768,768]{1,0:T(8,128)(2,1)} async-done(((bf16[96,768]{1,0:T(8,128)(2,1)}), bf16[768,768]{1,0:T(8,128)(2,1)}) %all-gather.3.cloned.1.call-update) | async-done | bytes 1179664 | tf_op jit(solution)/shard_map/all_gather | solution.py:35
  96.5 6.2 %fusion.13 = f32[768,1536]{1,0:T(8,128)} fusion(bf16[768,768]{1,0:T(8,128)(2,1)} %all-gather.3.cloned.1.call-done, bf16[1536,768]{1,0:T(8,128)(2,1)} %param.8), kind=kOutput, calls=%fused_computation.22 | convolution fusion | flops 1811939328 | bytes 8257536 | tf_op jit(solution)/shard_map/dot_general | solution.py:47
  102.7 0.0 copy-start.2
  102.7 0.0 reduce-scatter.5.cloned.1.call-update
  102.7 1.2 copy-done.2
  104.0 5.1 %fusion = bf16[1536,768]{0,1:T(8,128)(2,1)} fusion(bf16[768,768]{1,0:T(8,128)(2,1)S(1)} %copy-done.2, bf16[768,1536]{1,0:T(8,128)(2,1)} %param.5), kind=kOutput, calls=%fused_computation.2 | convolution fusion | flops 1814298624 | bytes 5898240 | tf_op jit(solution)/shard_map/dot_general | solution.py:41
  109.1 4.3 %copy.8 = bf16[1536,768]{1,0:T(8,128)(2,1)} copy(bf16[1536,768]{0,1:T(8,128)(2,1)} %fusion) | data formatting | bytes 4718592
  113.3 22.2 %all-gather.5.cloned.1.call-done = bf16[768,768]{1,0:T(8,128)(2,1)} async-done(((bf16[96,768]{1,0:T(8,128)(2,1)}), bf16[768,768]{1,0:T(8,128)(2,1)}) %all-gather.5.cloned.1.call-update) | async-done | bytes 1179664 | tf_op jit(solution)/shard_map/all_gather | solution.py:34
  135.5 4.7 %multiply_convert_fusion = bf16[768,1536]{1,0:T(8,128)(2,1)} fusion(bf16[768,768]{1,0:T(8,128)(2,1)} %all-gather.5.cloned.1.call-done, bf16[768,1536]{1,0:T(8,128)(2,1)S(1)} %copy-done), kind=kOutput, calls=%fused_computation | convolution fusion | flops 1814298624 | bytes 5898240 | tf_op jit(solution)/shard_map/dot_general | solution.py:37
  140.2 92.5 %reduce-scatter.5.cloned.1.call-done = f32[24,1536]{1,0:T(8,128)} async-done(((f32[768,1536]{1,0:T(8,128)}), f32[24,1536]{1,0:T(8,128)}) %reduce-scatter.5.cloned.1.call-update) | async-done | bytes 147472 | tf_op jit(solution)/shard_map/reduce_scatter | solution.py:46
  232.7 1.6 convert_element_type.23
Async XLA Ops:
  7.2 1.7 copy-start
  7.2 49.9 %reduce-scatter.3.cloned.1.call-start = ((), (), s32[]{:S(2)}) async-start(), calls=%async_computation.2 | async-start | bytes 2654208 | tf_op jit(solution)/shard_map/reduce_scatter | solution.py:25
  13.9 43.1 %copy-start.1 = (bf16[96,768]{1,0:T(8,128)(2,1)S(1)}, bf16[96,768]{1,0:T(8,128)(2,1)}, u32[]{:S(2)}) copy-start(bf16[96,768]{1,0:T(8,128)(2,1)} %param.7) | copy-start | bytes 442372
  14.0 82.5 %all-gather.3.cloned.1.call-start = ((), (), s32[]{:S(2)}) async-start(), calls=%async_computation.3 | async-start | bytes 1327104 | tf_op jit(solution)/shard_map/all_gather | solution.py:35
  59.0 76.6 %all-gather.5.cloned.1.call-start = ((), (), s32[]{:S(2)}) async-start(), calls=%async_computation.5 | async-start | bytes 1327104 | tf_op jit(solution)/shard_map/all_gather | solution.py:34
  59.7 173.0 %reduce-scatter.5.cloned.1.call-start = ((), (), s32[]{:S(2)}) async-start(), calls=%async_computation.4 | async-start | bytes 4866048 | tf_op jit(solution)/shard_map/reduce_scatter | solution.py:46
  102.7 1.3 copy-start.2
Sparse Core Ops, SparseCore 0:
  14.1 42.9 reduce-scatter.2
  59.4 37.0 all-gather.2
  98.3 37.2 all-gather.4
  139.4 93.2 reduce-scatter.4
where the time goes:
time: 242 us; the launch traced here: 241 us
  waiting for transfers between devices  195 us (81%)
  matrix products  21.1 us (9%)
  between operations  13.8 us (6%)
  local copies, waits for them, and re-layouts  7.13 us (3%)
  other arithmetic  3.43 us (1%)
    reduce_scatter x1, waiting for transfers between devices, per_device(): lax.psum_scatter(lax.dot_general(block, w_in, (((1,), (1,)), ((), ())), p...  92.5 us
    reduce_scatter x1, waiting for transfers between devices, per_device(): lax.psum_scatter(lax.dot_general(block, w_out, (((1,), (1,)), ((), ())),...  43 us
    all_gather x1, waiting for transfers between devices, per_device(): lax.all_gather(hid_share, 'col', axis=0, tiled=True)  36.7 us
    all_gather x1, waiting for transfers between devices, per_device(): lax.all_gather(local_act.astype(jnp.bfloat16), 'col', axis=0, tiled=True)  22.2 us
    unnamed x7, local copies, waits for them, and re-layouts  7.13 us
    dot_general x1, matrix products, per_device(): lax.dot_general(block, w_in, (((1,), (1,)), ((), ())), preferred_element_...  6.2 us
    dot_general x1, matrix products, per_device(): lax.dot_general(block, w_out, (((1,), (1,)), ((), ())), preferred_element...  5.1 us
    dot_general x1, matrix products, per_device(): lax.dot_general(inputs, hid_all, (((0,), (0,)), ((), ())), preferred_elem...  5.1 us
  transfers between devices with their start and end apart: 4, of which 4 were waited for; matrix products, arithmetic and copies ran while one was open for 8% of the time, Pallas kernels for 0%

commit v1 on v0

v1 whole, which is shorter than its diff:
```python
import functools
import math

import jax
import jax.numpy as jnp
from jax import lax
from jax.experimental import pallas as pl
from jax.experimental.pallas import tpu as pltpu
from jax.sharding import PartitionSpec as P

coef_c = math.sqrt(2.0 / math.pi)
F32, BF16 = jnp.float32, jnp.bfloat16
MESH = pl.DeviceIdType.MESH

TOK, HID, DM = 768, 768, 1536
NZ, CH, PR = 8, 96, 48
BLK = 24


def gelu_parts(hval):
    tval = jnp.tanh(coef_c * (hval + 0.044715 * hval * hval * hval))
    activ = 0.5 * hval * (1.0 + tval)
    deriv = 0.5 * (1.0 + tval) + 0.5 * hval * (1.0 - tval * tval) * coef_c * (
        1.0 + 3.0 * 0.044715 * hval * hval
    )
    return activ, deriv


def dot_nt(a, b):
    return lax.dot_general(a, b, (((1,), (1,)), ((), ())), preferred_element_type=F32)


def dot_nn(a, b):
    return lax.dot_general(a, b, (((1,), (0,)), ((), ())), preferred_element_type=F32)


def dot_tn(a, b):
    return lax.dot_general(a, b, (((0,), (0,)), ((), ())), preferred_element_type=F32)


def kernel(
    inp_h, og_h, pa_h, win_h, wout_h,
    gi_ref, gwi_h, gwo_h,
    inp, og, pa, win, wout, inpt,
    hid, act, deriv, pbuf,
    rs_s, rs_r,
    gip, pair_r, summed,
    s1, r1, t1, s2, r2,
    gwi, gwo,
    ld_sem, og_sem, st_sem,
    rs_ss, rs_rs, hg_ss, hg_rs, ag_ss, ag_rs, pr_ss, pr_rs,
    x1_ss, x1_rs, x2_ss, x2_rs,
):
    row = lax.axis_index("row")
    z = lax.axis_index("col")
    core = lax.rem(row, 2)
    chip = lax.div(row, 2)
    x = lax.rem(chip, 4)
    y = lax.div(chip, 4)
    scale = 1.0 / math.sqrt(TOK)

    def at(yy, xx, cc):
        return (yy * 4 + xx) * 2 + cc

    def wrap(v, n):
        return lax.rem(v + n, n)

    z_dev = [(row, wrap(z + 1, NZ)), (row, wrap(z - 1, NZ))]
    x_dev = [(at(y, wrap(x + 1, 4), core), z), (at(y, wrap(x - 1, 4), core), z)]
    y_dev = [(at(wrap(y + 1, 4), x, core), z), (at(wrap(y - 1, 4), x, core), z)]
    partner = (at(y, x, 1 - core), z)

    def remote(src, dst, ss, rs, dev):
        return pltpu.make_async_remote_copy(
            src_ref=src, dst_ref=dst, send_sem=ss, recv_sem=rs, device_id=dev, device_id_type=MESH
        )

    def rows(start, size, mult=8):
        return pl.ds(pl.multiple_of(start, mult), size)

    def zc(k):
        return wrap(z + k, NZ)

    def load(src, dst, sem):
        c = pltpu.make_async_copy(src, dst, sem)
        c.start()
        return c

    ld_pa = load(pa_h, pa, ld_sem.at[0])
    order = [4, 3, -3, 2, -2, 1, -1, 0]
    ld_og = {}

    def load_og(n):
        k = order[n]
        ds = rows(zc(k) * CH, CH, 16)
        ld_og[k] = load(og_h.at[ds, :], og.at[ds, :], og_sem.at[n])

    load_og(0)
    ld_wout = load(wout_h, wout, ld_sem.at[1])
    for n in range(1, 8):
        load_og(n)
    ld_win = load(win_h, win, ld_sem.at[2])
    ld_inp = load(inp_h, inp, ld_sem.at[3])

    barrier = pltpu.get_barrier_semaphore()
    peers = z_dev + x_dev + y_dev + [partner]
    for dev in peers:
        pl.semaphore_signal(barrier, inc=1, device_id=dev, device_id_type=MESH)

    ld_pa.wait()
    activ, dv = gelu_parts(pa[...].astype(F32))
    act[rows(z * CH, CH, 16), :] = activ.astype(BF16)
    deriv[...] = dv

    pl.semaphore_wait(barrier, len(peers))

    def ring_piece(buf, ss, rs, d, s, p):
        src_chunk = zc(-s) if d == 0 else zc(s)
        ds = rows(src_chunk * CH + p * PR, PR, 16)
        i = 2 * s + (p if s < 3 else 0)
        return remote(buf.at[ds, :], buf.at[ds, :], ss.at[d, i], rs.at[d, i], z_dev[d])

    def far_piece(d):
        return 0 if d == 0 else 1

    sends = []

    def go(c):
        c.start()
        sends.append(c)
        return c

    ag = {}

    def act_send(d, s, p):
        ag[d, s, p] = go(ring_piece(act, ag_ss, ag_rs, d, s, p))

    for p in range(2):
        for d in range(2):
            act_send(d, 0, p)

    def partial(k, slot):
        ld_og[k].wait()
        a = og[rows(zc(k) * CH, CH, 16), :]
        for n in range(3):
            cs = slice(n * 256, n * 256 + 256)
            pbuf[slot, :, cs] = dot_nt(a, wout[cs, :])

    rs = {}

    def rs_send(d, s, p, value):
        i = 0 if s == 0 else 2 * s - 1 + p
        rs_s[d, i] = value.astype(BF16)
        rs[d, s, p] = go(remote(rs_s.at[d, i], rs_r.at[d, i], rs_ss.at[d, i], rs_rs.at[d, i], z_dev[d]))

    def rs_recv(d, s, p):
        i = 0 if s == 0 else 2 * s - 1 + p
        rs[d, s, p].wait_recv()
        return rs_r[d, i].astype(F32)

    def half(p):
        return slice(p * PR, p * PR + PR)

    ld_wout.wait()
    partial(4, 0)
    for d in range(2):
        p = far_piece(d)
        rs_send(d, 0, p, pbuf[0, half(p), :])
    for s in range(1, 4):
        for d in range(2):
            partial(4 - s if d == 0 else s - 4, d)
            if s == 1:
                p = 1 - far_piece(d)
                rs_send(d, s, p, pbuf[d, half(p), :])
        if s == 1:
            for d in range(2):
                p = far_piece(d)
                rs_send(d, s, p, pbuf[d, half(p), :] + rs_recv(d, 0, p))
        else:
            for q in range(2):
                for d in range(2):
                    p = 1 - far_piece(d) if q == 0 else far_piece(d)
                    rs_send(d, s, p, pbuf[d, half(p), :] + rs_recv(d, s - 1, p))
        if s == 2:
            ld_inp.wait()
        if s >= 2:
            for n in range(3):
                cs = slice((s - 2) * 768 + n * 256, (s - 2) * 768 + n * 256 + 256)
                inpt[cs, :] = inp[:, cs].T

    for d in range(2):
        ag[d, 0, 0].wait_recv()
        act_send(d, 1, 0)

    partial(0, 0)
    hg = {}

    def hid_send(d, s, p):
        hg[d, s, p] = go(ring_piece(hid, hg_ss, hg_rs, d, s, p))

    for p in range(2):
        total = pbuf[0, half(p), :] + rs_recv(0, 3, p) + rs_recv(1, 3, p)
        hid[rows(z * CH + p * PR, PR, 16), :] = (total * deriv[half(p), :]).astype(BF16)
        for d in range(2):
            hid_send(d, 0, p)

    pair = []

    def grad_chunk(k):
        c = zc(k)
        a = hid[rows(c * CH, CH, 16), :]
        for n in range(6):
            cs = slice(n * 256, n * 256 + 256)
            gip[rows(c * CH, CH, 8), cs] = dot_nt(a, win[cs, :])
        i = len(pair) // 2
        for j in range(2):
            src = gip.at[rows(c * CH + (2 * j + 1 - core) * BLK, BLK, 8), :]
            cp = go(remote(src, pair_r.at[i, j], pr_ss.at[i, j], pr_rs.at[i, j], partner))
            pair.append(cp)
        return i

    def pair_sum(k, i):
        c = zc(k)
        for j in range(2):
            pair[2 * i + j].wait_recv()
            own = gip[rows(c * CH + (2 * j + core) * BLK, BLK, 8), :]
            summed[rows((2 * c + j) * BLK, BLK, 8), :] = own + pair_r[i, j]

    ld_win.wait()
    done = [0]
    idx = {0: grad_chunk(0)}
    for s in range(3):
        for p in range(2):
            for d in range(2):
                hg[d, s, p].wait_recv()
                if s < 2 or p == far_piece(d):
                    hid_send(d, s + 1, p)
        if s == 2:
            for d in range(2):
                ag[d, 0, 1].wait_recv()
                act_send(d, 1, 1)
        for k in (-(s + 1), s + 1):
            idx[k] = grad_chunk(k)
        for k in done:
            pair_sum(k, idx[k])
        done = [-(s + 1), s + 1]
    for d in range(2):
        ag[d, 1, 0].wait_recv()
        act_send(d, 2, 0)
    for d in range(2):
        hg[d, 3, far_piece(d)].wait_recv()
    idx[4] = grad_chunk(4)
    for k in done + [4]:
        pair_sum(k, idx[k])
    for d in range(2):
        ag[d, 1, 1].wait_recv()
        act_send(d, 2, 1)

    me = [(x, y), (y, x)]
    devs = [(x_dev, y_dev), (y_dev, x_dev)]

    def own1(h, dest, p):
        if h == 0:
            return jnp.concatenate(
                [summed[rows((q * 4 + dest) * BLK, BLK, 8), :HID] for q in (2 * p, 2 * p + 1)], axis=0
            )
        return summed[rows(dest * 4 * BLK + p * PR, PR, 8), HID:]

    c1, c2 = {}, {}

    def send1(h, d, i, value):
        s1[h, d, i] = value.astype(BF16)
        c1[h, d, i] = go(
            remote(s1.at[h, d, i], r1.at[h, d, i], x1_ss.at[h, d, i], x1_rs.at[h, d, i], devs[h][0][d])
        )

    def recv1(h, d, i):
        c1[h, d, i].wait_recv()
        return r1[h, d, i].astype(F32)

    def own2(h, dest, p):
        return t1[h, rows(dest * BLK, BLK, 8), p * 384 : p * 384 + 384]

    def send2(h, d, i, value):
        s2[h, d, i] = value
        c2[h, d, i] = go(
            remote(s2.at[h, d, i], r2.at[h, d, i], x2_ss.at[h, d, i], x2_rs.at[h, d, i], devs[h][1][d])
        )

    def recv2(h, d, i):
        c2[h, d, i].wait_recv()
        return r2[h, d, i]

    stores = []

    def store(src, dst, i):
        c = pltpu.make_async_copy(src, dst, st_sem.at[i])
        c.start()
        stores.append(c)

    def grad_w_in_tile(i):
        rs_ = slice(i * 256, i * 256 + 256)
        gwi[rs_, :] = (dot_nn(inpt[rs_, :], hid[...]) * scale).astype(BF16)
        store(gwi.at[rs_, :], gwi_h.at[rs_, :], i)

    def grad_w_out_tile(i):
        rs_ = slice(i * 256, i * 256 + 256)
        gwo[rs_, :] = (dot_tn(act[:, rs_], og[...]) * scale).astype(BF16)
        store(gwo.at[rs_, :], gwo_h.at[rs_, :], 6 + i)

    step = (1, -1)
    for h in range(2):
        for d in range(2):
            send1(h, d, 0, own1(h, wrap(me[h][0] + 2, 4), far_piece(d)))
    for h in range(2):
        for d in range(2):
            send1(h, d, 1, own1(h, wrap(me[h][0] + step[d], 4), 1 - far_piece(d)))
    grad_w_in_tile(0)
    grad_w_in_tile(1)
    for h in range(2):
        for d in range(2):
            p = far_piece(d)
            send1(h, d, 2, own1(h, wrap(me[h][0] + step[d], 4), p) + recv1(h, d, 0))
    for d in range(2):
        p = far_piece(d)
        ag[d, 2, p].wait_recv()
        act_send(d, 3, p)
    grad_w_in_tile(2)
    grad_w_in_tile(3)
    for h in range(2):
        for p in range(2):
            fwd = recv1(h, 0, 2 if p == 0 else 1)
            bwd = recv1(h, 1, 1 if p == 0 else 2)
            t1[h, half(p), :] = own1(h, me[h][0], p) + fwd + bwd
    for h in range(2):
        for d in range(2):
            send2(h, d, 0, own2(h, wrap(me[h][1] + 2, 4), far_piece(d)))
    for h in range(2):
        for d in range(2):
            send2(h, d, 1, own2(h, wrap(me[h][1] + step[d], 4), 1 - far_piece(d)))
    grad_w_in_tile(4)
    grad_w_in_tile(5)
    for h in range(2):
        for d in range(2):
            p = far_piece(d)
            send2(h, d, 2, own2(h, wrap(me[h][1] + step[d], 4), p) + recv2(h, d, 0))
    for d in range(2):
        ag[d, 2, 1 - far_piece(d)].wait_recv()
        ag[d, 3, far_piece(d)].wait_recv()
    for i in range(3):
        grad_w_out_tile(i)
    for h in range(2):
        for p in range(2):
            fwd = recv2(h, 0, 2 if p == 0 else 1)
            bwd = recv2(h, 1, 1 if p == 0 else 2)
            c0 = h * HID + p * 384
            gi_ref[:, c0 : c0 + 384] = (own2(h, me[h][1], p) + fwd + bwd).astype(BF16)

    for c in sends:
        c.wait_send()
    for c in stores:
        c.wait()


def per_device(inputs, out_grad, pre_act, w_in, w_out):
    any_spec = pl.BlockSpec(memory_space=pl.ANY)
    vm = pltpu.VMEM
    dma = pltpu.SemaphoreType.DMA
    return pl.pallas_call(
        kernel,
        out_shape=(
            jax.ShapeDtypeStruct((BLK, DM), BF16),
            jax.ShapeDtypeStruct((DM, HID), BF16),
            jax.ShapeDtypeStruct((HID, DM), BF16),
        ),
        in_specs=[any_spec] * 5,
        out_specs=(pl.BlockSpec(memory_space=pltpu.VMEM), any_spec, any_spec),
        scratch_shapes=[
            vm((TOK, DM), BF16), vm((TOK, DM), BF16), vm((CH, HID), BF16),
            vm((DM, HID), BF16), vm((HID, DM), BF16), vm((DM, TOK), BF16),
            vm((TOK, HID), BF16), vm((TOK, HID), BF16), vm((CH, HID), F32), vm((2, CH, HID), F32),
            vm((2, 7, PR, HID), BF16), vm((2, 7, PR, HID), BF16),
            vm((TOK, DM), F32), vm((8, 2, BLK, DM), F32), vm((TOK // 2, DM), F32),
            vm((2, 2, 3, PR, HID), BF16), vm((2, 2, 3, PR, HID), BF16), vm((2, CH, HID), F32),
            vm((2, 2, 3, BLK, 384), F32), vm((2, 2, 3, BLK, 384), F32),
            vm((DM, HID), BF16), vm((HID, DM), BF16),
            dma((4,)), dma((8,)), dma((9,)),
            dma((2, 7)), dma((2, 7)), dma((2, 7)), dma((2, 7)), dma((2, 7)), dma((2, 7)),
            dma((8, 2)), dma((8, 2)),
            dma((2, 2, 3)), dma((2, 2, 3)), dma((2, 2, 3)), dma((2, 2, 3)),
        ],
        compiler_params=pltpu.CompilerParams(
            collective_id=0, has_side_effects=True, vmem_limit_bytes=60 * 1024 * 1024
        ),
        name="ffn_backward",
    )(inputs, out_grad, pre_act, w_in, w_out)


def solution(mesh):
    placed = (P(None, "col"), P(None, "col"), P("col", "row"), P("col", "row"), P("row", "col"))
    return jax.shard_map(
        per_device,
        mesh=mesh,
        in_specs=placed,
        out_specs=(P("row", "col"), P("col", "row"), P("row", "col")),
        check_vma=False,
    )
```

time: 242 us -> 72 us (0.30)
  waiting for transfers between devices: 195 us -> 0 us
  Pallas kernels: 0 us -> 65 us
  matrix products: 21.1 us -> 0 us
  between operations: 13.8 us -> 0.64 us
  other arithmetic: 3.43 us -> 0 us
    reduce_scatter x2 -> x0, waiting for transfers between devices: 136 us -> none  [the longest x1 92.5 us: per_device(): lax.psum_scatter(lax.dot_general(block, w_in, (((1,), (1,)), ((), ())), p...]
    pallas_call x0 -> x1, Pallas kernels: none -> 65 us  [per_device(): pl.pallas_call(kernel, out_shape=(jax.ShapeDtypeStruct((BLK, DM), BF16),...]
    all_gather x2 -> x0, waiting for transfers between devices: 59 us -> none  [the longest x1 36.7 us: per_device(): lax.all_gather(hid_share, 'col', axis=0, tiled=True)]
    dot_general x4 -> x0, matrix products: 21.1 us -> none  [the longest x1 6.2 us: per_device(): lax.dot_general(block, w_in, (((1,), (1,)), ((), ())), preferred_element_...]
    convert_element_type x2 -> x0, other arithmetic: 3.43 us -> none  [the longest x1 1.88 us: per_device(): local_act.astype(jnp.bfloat16)]
    unnamed x7 -> x5, local copies, waits for them, and re-layouts: 7.13 us -> 6.3 us
  transfers between devices with their start and end apart: 4 -> 0, of which waited for: 4 -> 0; matrix products, arithmetic and copies ran while one was open for 8% -> 0% of each run, Pallas kernels for 0% -> 0%
where the time goes in v1:
time: 72 us; the launch traced here: 71.9 us
  Pallas kernels  65 us (90%)
  local copies, waits for them, and re-layouts  6.3 us (9%)
    pallas_call x1, Pallas kernels, per_device(): pl.pallas_call(kernel, out_shape=(jax.ShapeDtypeStruct((BLK, DM), BF16),...  65 us
    unnamed x5, local copies, waits for them, and re-layouts  6.3 us

profile of v1, /device:TPU:1, one launch (start us, length us, event | category | flops | bytes accessed | tf_op | source)
XLA Modules:
  0.0 71.9 jit_solution(6923733319357447509)
XLA Ops:
  0.6 65.0 %ffn_backward.1 = (bf16[24,1536]{1,0:T(8,128)(2,1)}, bf16[1536,768]{1,0:T(8,128)(2,1)}, bf16[768,1536]{1,0:T(8,128)(2,1)}) custom-call(bf16[768,1536]{1,0:T(8,128)(2,1)} %inp_h.1, bf16[768,1536]{1,0:T(8,128)(2,1)} %og_h.1, bf16[96,768]{1,0:T(8,128)(2,1)} %pa_h.1, bf16[1536,768]{1,0:T(8,128)(2,1)} %win_h.1, bf16[768,1536]{1,0:T(8,128)(2,1)} %wout_h.1), custom_call_target="tpu_custom_call" | custom-call | tf_op jit(solution)/shard_map/ffn_backward/pallas_call | solution.py:369
  65.6 1.5 %copy.11 = bf16[24,1536]{1,0:T(8,128)(2,1)} copy(bf16[24,1536]{1,0:T(8,128)(2,1)} %get-tuple-element.6) | data formatting | bytes 147456
  67.1 0.0 copy-start
  67.1 3.4 %copy.12 = bf16[1536,768]{1,0:T(8,128)(2,1)} copy(bf16[1536,768]{1,0:T(8,128)(2,1)} %get-tuple-element.7) | data formatting | bytes 4718592
  70.5 0.0 copy-done
  70.5 1.4 %copy.13 = bf16[768,1536]{1,0:T(8,128)(2,1)} copy(bf16[768,1536]{1,0:T(8,128)(2,1)S(1)} %copy-done) | data formatting | bytes 4718592
Async XLA Ops:
  67.1 3.4 %copy-start = (bf16[768,1536]{1,0:T(8,128)(2,1)S(1)}, bf16[768,1536]{1,0:T(8,128)(2,1)}, u32[]{:S(2)}) copy-start(bf16[768,1536]{1,0:T(8,128)(2,1)} %get-tuple-element.8) | copy-start | bytes 7077892

commit v2 on v1

--- a/solution.py
+++ b/solution.py
@@ -14,6 +14,7 @@
 
 TOK, HID, DM = 768, 768, 1536
 NZ, CH, PR = 8, 96, 48
+PC = 384
 BLK = 24
 
 
@@ -112,17 +113,6 @@
     act[rows(z * CH, CH, 16), :] = activ.astype(BF16)
     deriv[...] = dv
 
-    pl.semaphore_wait(barrier, len(peers))
-
-    def ring_piece(buf, ss, rs, d, s, p):
-        src_chunk = zc(-s) if d == 0 else zc(s)
-        ds = rows(src_chunk * CH + p * PR, PR, 16)
-        i = 2 * s + (p if s < 3 else 0)
-        return remote(buf.at[ds, :], buf.at[ds, :], ss.at[d, i], rs.at[d, i], z_dev[d])
-
-    def far_piece(d):
-        return 0 if d == 0 else 1
-
     sends = []
 
     def go(c):
@@ -130,131 +120,171 @@
         sends.append(c)
         return c
 
+    def far_piece(d):
+        return 0 if d == 0 else 1
+
+    def chunk_at(d, s):
+        return zc(-s) if d == 0 else zc(s)
+
     ag = {}
 
     def act_send(d, s, p):
-        ag[d, s, p] = go(ring_piece(act, ag_ss, ag_rs, d, s, p))
-
-    for p in range(2):
-        for d in range(2):
-            act_send(d, 0, p)
-
-    def partial(k, slot):
+        ds = rows(chunk_at(d, s) * CH + p * PR, PR, 16)
+        i = 2 * s + (p if s < 3 else 0)
+        ag[d, s, p] = go(remote(act.at[ds, :], act.at[ds, :], ag_ss.at[d, i], ag_rs.at[d, i], z_dev[d]))
+
+    def partial(k):
         ld_og[k].wait()
         a = og[rows(zc(k) * CH, CH, 16), :]
         for n in range(3):
             cs = slice(n * 256, n * 256 + 256)
-            pbuf[slot, :, cs] = dot_nt(a, wout[cs, :])
+            pbuf[k + 3, :, cs] = dot_nt(a, wout[cs, :])
+
+    pieces = [(0, 0), (1, 0), (0, 1), (1, 1)]
+
+    def piece_id(s, q):
+        return q[1] if s == 0 else 4 * s - 2 + 2 * q[0] + q[1]
+
+    def fwd_id(s, q):
+        return 4 * s + (2 * q[0] + q[1] if s < 3 else q[1])
+
+    def part(q):
+        return slice(q[0] * PR, q[0] * PR + PR), slice(q[1] * PC, q[1] * PC + PC)
 
     rs = {}
 
-    def rs_send(d, s, p, value):
-        i = 0 if s == 0 else 2 * s - 1 + p
+    def rs_send(d, s, q):
+        i = piece_id(s, q)
+        r, c = part(q)
+        value = pbuf[(4 - s if d == 0 else (s - 4 if s else 4)) + 3, r, c]
+        if (d, s - 1, q) in rs:
+            value = value + rs_recv(d, s - 1, q)
         rs_s[d, i] = value.astype(BF16)
-        rs[d, s, p] = go(remote(rs_s.at[d, i], rs_r.at[d, i], rs_ss.at[d, i], rs_rs.at[d, i], z_dev[d]))
-
-    def rs_recv(d, s, p):
-        i = 0 if s == 0 else 2 * s - 1 + p
-        rs[d, s, p].wait_recv()
-        return rs_r[d, i].astype(F32)
+        rs[d, s, q] = go(remote(rs_s.at[d, i], rs_r.at[d, i], rs_ss.at[d, i], rs_rs.at[d, i], z_dev[d]))
+
+    def rs_recv(d, s, q):
+        rs[d, s, q].wait_recv()
+        return rs_r[d, piece_id(s, q)].astype(F32)
 
     def half(p):
         return slice(p * PR, p * PR + PR)
 
+    def transpose(n):
+        cs = slice(n * 256, n * 256 + 256)
+        inpt[cs, :] = inp[:, cs].T
+
     ld_wout.wait()
-    partial(4, 0)
-    for d in range(2):
-        p = far_piece(d)
-        rs_send(d, 0, p, pbuf[0, half(p), :])
-    for s in range(1, 4):
-        for d in range(2):
-            partial(4 - s if d == 0 else s - 4, d)
-            if s == 1:
-                p = 1 - far_piece(d)
-                rs_send(d, s, p, pbuf[d, half(p), :])
-        if s == 1:
+    partial(4)
+    partial(3)
+    partial(-3)
+    pl.semaphore_wait(barrier, len(peers))
+    for c in range(2):
+        for d in range(2):
+            rs_send(d, 0, (far_piece(d), c))
+    for c in range(2):
+        for d in range(2):
+            rs_send(d, 1, (1 - far_piece(d), c))
+    partial(2)
+    partial(-2)
+    for c in range(2):
+        for d in range(2):
+            rs_send(d, 1, (far_piece(d), c))
+    partial(1)
+    partial(-1)
+    for s in (2, 3):
+        for far in range(2):
+            for c in range(2):
+                for d in range(2):
+                    rs_send(d, s, (far_piece(d) if far else 1 - far_piece(d), c))
+            if s == 2 and far == 0:
+                partial(0)
+            if s == 2 and far == 1:
+                ld_inp.wait()
+                for n in range(3):
+                    transpose(n)
+            if s == 3 and far == 0:
+                for n in range(3, 6):
+                    transpose(n)
+
+    for d in range(2):
+        act_send(d, 0, 0)
+
+    hg = {}
+
+    def hid_send(d, s, q):
+        ds = rows(chunk_at(d, s) * CH + q[0] * PR, PR, 16)
+        src = hid.at[ds, q[1] * PC : q[1] * PC + PC]
+        i = fwd_id(s, q)
+        hg[d, s, q] = go(remote(src, src, hg_ss.at[d, i], hg_rs.at[d, i], z_dev[d]))
+
+    for q in pieces:
+        r, c = part(q)
+        total = pbuf[3, r, c] + rs_recv(0, 3, q) + rs_recv(1, 3, q)
+        hid[rows(z * CH + q[0] * PR, PR, 16), c] = (total * deriv[r, c]).astype(BF16)
+        for d in range(2):
+            hid_send(d, 0, q)
+
+    pair = {}
+
+    def grad_half(k, m):
+        c = zc(k)
+        a = hid[rows(c * CH, CH, 16), :]
+        for n in range(3 * m, 3 * m + 3):
+            cs = slice(n * 256, n * 256 + 256)
+            gip[rows(c * CH, CH, 8), cs] = dot_nt(a, win[cs, :])
+        if m == 1:
+            for j in range(2):
+                i = k + 3
+                src = gip.at[rows(c * CH + (2 * j + 1 - core) * BLK, BLK, 8), :]
+                pair[k, j] = go(remote(src, pair_r.at[i, j], pr_ss.at[i, j], pr_rs.at[i, j], partner))
+
+    def pair_sum(k):
+        c = zc(k)
+        for j in range(2):
+            pair[k, j].wait_recv()
+            own = gip[rows(c * CH + (2 * j + core) * BLK, BLK, 8), :]
+            summed[rows((2 * c + j) * BLK, BLK, 8), :] = own + pair_r[k + 3, j]
+
+    ld_win.wait()
+    work = [(grad_half, 0, 0), (grad_half, 0, 1)]
+
+    def tick():
+        if work:
+            item = work.pop(0)
+            item[0](*item[1:])
+
+    last = [0]
+    for s in range(3):
+        for q in pieces:
             for d in range(2):
-                p = far_piece(d)
-                rs_send(d, s, p, pbuf[d, half(p), :] + rs_recv(d, 0, p))
-        else:
-            for q in range(2):
-                for d in range(2):
-                    p = 1 - far_piece(d) if q == 0 else far_piece(d)
-                    rs_send(d, s, p, pbuf[d, half(p), :] + rs_recv(d, s - 1, p))
-        if s == 2:
-            ld_inp.wait()
-        if s >= 2:
-            for n in range(3):
-                cs = slice((s - 2) * 768 + n * 256, (s - 2) * 768 + n * 256 + 256)
-                inpt[cs, :] = inp[:, cs].T
-
-    for d in range(2):
+                hg[d, s, q].wait_recv()
+                if s < 2 or q[0] == far_piece(d):
+                    hid_send(d, s + 1, q)
+            tick()
+        while work:
+            tick()
+        for k in last:
+            work.append((pair_sum, k))
+        last = [-(s + 1), s + 1]
+        for k in last:
+            work += [(grad_half, k, 0), (grad_half, k, 1)]
+        work.sort(key=lambda w: w[0] is pair_sum)
+    for d in range(2):
+        act_send(d, 0, 1)
         ag[d, 0, 0].wait_recv()
         act_send(d, 1, 0)
-
-    partial(0, 0)
-    hg = {}
-
-    def hid_send(d, s, p):
-        hg[d, s, p] = go(ring_piece(hid, hg_ss, hg_rs, d, s, p))
-
-    for p in range(2):
-        total = pbuf[0, half(p), :] + rs_recv(0, 3, p) + rs_recv(1, 3, p)
-        hid[rows(z * CH + p * PR, PR, 16), :] = (total * deriv[half(p), :]).astype(BF16)
-        for d in range(2):
-            hid_send(d, 0, p)
-
-    pair = []
-
-    def grad_chunk(k):
-        c = zc(k)
-        a = hid[rows(c * CH, CH, 16), :]
-        for n in range(6):
-            cs = slice(n * 256, n * 256 + 256)
-            gip[rows(c * CH, CH, 8), cs] = dot_nt(a, win[cs, :])
-        i = len(pair) // 2
-        for j in range(2):
-            src = gip.at[rows(c * CH + (2 * j + 1 - core) * BLK, BLK, 8), :]
-            cp = go(remote(src, pair_r.at[i, j], pr_ss.at[i, j], pr_rs.at[i, j], partner))
-            pair.append(cp)
-        return i
-
-    def pair_sum(k, i):
-        c = zc(k)
-        for j in range(2):
-            pair[2 * i + j].wait_recv()
-            own = gip[rows(c * CH + (2 * j + core) * BLK, BLK, 8), :]
-            summed[rows((2 * c + j) * BLK, BLK, 8), :] = own + pair_r[i, j]
-
-    ld_win.wait()
-    done = [0]
-    idx = {0: grad_chunk(0)}
-    for s in range(3):
-        for p in range(2):
-            for d in range(2):
-                hg[d, s, p].wait_recv()
-                if s < 2 or p == far_piece(d):
-                    hid_send(d, s + 1, p)
-        if s == 2:
-            for d in range(2):
-                ag[d, 0, 1].wait_recv()
-                act_send(d, 1, 1)
-        for k in (-(s + 1), s + 1):
-            idx[k] = grad_chunk(k)
-        for k in done:
-            pair_sum(k, idx[k])
-        done = [-(s + 1), s + 1]
-    for d in range(2):
-        ag[d, 1, 0].wait_recv()
-        act_send(d, 2, 0)
-    for d in range(2):
-        hg[d, 3, far_piece(d)].wait_recv()
-    idx[4] = grad_chunk(4)
-    for k in done + [4]:
-        pair_sum(k, idx[k])
-    for d in range(2):
-        ag[d, 1, 1].wait_recv()
-        act_send(d, 2, 1)
+    while work:
+        tick()
+    for c in range(2):
+        for d in range(2):
+            hg[d, 3, (far_piece(d), c)].wait_recv()
+    grad_half(4, 0)
+    grad_half(4, 1)
+    for d in range(2):
+        ag[d, 0, 1].wait_recv()
+        act_send(d, 1, 1)
+    for k in last + [4]:
+        pair_sum(k)
 
     me = [(x, y), (y, x)]
     devs = [(x_dev, y_dev), (y_dev, x_dev)]
@@ -315,6 +345,9 @@
     for h in range(2):
         for d in range(2):
             send1(h, d, 1, own1(h, wrap(me[h][0] + step[d], 4), 1 - far_piece(d)))
+    for d in range(2):
+        ag[d, 1, 0].wait_recv()
+        act_send(d, 2, 0)
     grad_w_in_tile(0)
     grad_w_in_tile(1)
     for h in range(2):
@@ -322,9 +355,8 @@
             p = far_piece(d)
             send1(h, d, 2, own1(h, wrap(me[h][0] + step[d], 4), p) + recv1(h, d, 0))
     for d in range(2):
-        p = far_piece(d)
-        ag[d, 2, p].wait_recv()
-        act_send(d, 3, p)
+        ag[d, 1, 1].wait_recv()
+        act_send(d, 2, 1)
     grad_w_in_tile(2)
     grad_w_in_tile(3)
     for h in range(2):
@@ -340,6 +372,10 @@
             send2(h, d, 1, own2(h, wrap(me[h][1] + step[d], 4), 1 - far_piece(d)))
     grad_w_in_tile(4)
     grad_w_in_tile(5)
+    for d in range(2):
+        p = far_piece(d)
+        ag[d, 2, p].wait_recv()
+        act_send(d, 3, p)
     for h in range(2):
         for d in range(2):
             p = far_piece(d)
@@ -362,30 +398,49 @@
         c.wait()
 
 
+def finish(gi_t, gwi_t, gwo_t, gi, gwi, gwo, gi_v, gwi_v, gwo_v, in_sem, out_sem):
+    jobs = [(gi_t, gi_v, gi)]
+    for n in range(3):
+        for t, v, o in ((gwi_t, gwi_v, gwi), (gwo_t, gwo_v, gwo)):
+            size = t.shape[0] // 3
+            ds = slice(n * size, n * size + size)
+            jobs.append((t.at[ds, :], v.at[ds, :], o.at[ds, :]))
+    ins = [pltpu.make_async_copy(t, v, in_sem.at[i]) for i, (t, v, o) in enumerate(jobs)]
+    outs = [pltpu.make_async_copy(v, o, out_sem.at[i]) for i, (t, v, o) in enumerate(jobs)]
+    for c in ins:
+        c.start()
+    for c, o in zip(ins, outs):
+        c.wait()
+        o.start()
+    for o in outs:
+        o.wait()
+
+
 def per_device(inputs, out_grad, pre_act, w_in, w_out):
     any_spec = pl.BlockSpec(memory_space=pl.ANY)
     vm = pltpu.VMEM
     dma = pltpu.SemaphoreType.DMA
-    return pl.pallas_call(
+    shapes = (
+        jax.ShapeDtypeStruct((BLK, DM), BF16),
+        jax.ShapeDtypeStruct((DM, HID), BF16),
+        jax.ShapeDtypeStruct((HID, DM), BF16),
+    )
+    results = pl.pallas_call(
         kernel,
-        out_shape=(
-            jax.ShapeDtypeStruct((BLK, DM), BF16),
-            jax.ShapeDtypeStruct((DM, HID), BF16),
-            jax.ShapeDtypeStruct((HID, DM), BF16),
-        ),
+        out_shape=shapes,
         in_specs=[any_spec] * 5,
         out_specs=(pl.BlockSpec(memory_space=pltpu.VMEM), any_spec, any_spec),
         scratch_shapes=[
             vm((TOK, DM), BF16), vm((TOK, DM), BF16), vm((CH, HID), BF16),
             vm((DM, HID), BF16), vm((HID, DM), BF16), vm((DM, TOK), BF16),
-            vm((TOK, HID), BF16), vm((TOK, HID), BF16), vm((CH, HID), F32), vm((2, CH, HID), F32),
-            vm((2, 7, PR, HID), BF16), vm((2, 7, PR, HID), BF16),
+            vm((TOK, HID), BF16), vm((TOK, HID), BF16), vm((CH, HID), F32), vm((8, CH, HID), F32),
+            vm((2, 14, PR, PC), BF16), vm((2, 14, PR, PC), BF16),
             vm((TOK, DM), F32), vm((8, 2, BLK, DM), F32), vm((TOK // 2, DM), F32),
             vm((2, 2, 3, PR, HID), BF16), vm((2, 2, 3, PR, HID), BF16), vm((2, CH, HID), F32),
             vm((2, 2, 3, BLK, 384), F32), vm((2, 2, 3, BLK, 384), F32),
             vm((DM, HID), BF16), vm((HID, DM), BF16),
             dma((4,)), dma((8,)), dma((9,)),
-            dma((2, 7)), dma((2, 7)), dma((2, 7)), dma((2, 7)), dma((2, 7)), dma((2, 7)),
+            dma((2, 14)), dma((2, 14)), dma((2, 14)), dma((2, 14)), dma((2, 7)), dma((2, 7)),
             dma((8, 2)), dma((8, 2)),
             dma((2, 2, 3)), dma((2, 2, 3)), dma((2, 2, 3)), dma((2, 2, 3)),
         ],
@@ -394,6 +449,16 @@
         ),
         name="ffn_backward",
     )(inputs, out_grad, pre_act, w_in, w_out)
+    return pl.pallas_call(
+        finish,
+        out_shape=shapes,
+        in_specs=[any_spec] * 3,
+        out_specs=(any_spec,) * 3,
+        scratch_shapes=[
+            vm((BLK, DM), BF16), vm((DM, HID), BF16), vm((HID, DM), BF16), dma((7,)), dma((7,)),
+        ],
+        name="finish",
+    )(*results)
 
 
 def solution(mesh):

time: 72 us -> 69.3 us (0.962)
  local copies, waits for them, and re-layouts: 6.3 us -> 0 us
  Pallas kernels: 65 us -> 68.6 us
    unnamed x5 -> x0, local copies, waits for them, and re-layouts: 6.3 us -> none
    pallas_call x1 -> x2, Pallas kernels: 65 us -> 68.6 us  [the longest x1 64.4 us: per_device(): pl.pallas_call(kernel, out_shape=shapes, in_specs=[any_spec] * 5, out_spe...]
where the time goes in v2:
time: 69.3 us; the launch traced here: 69.2 us
  Pallas kernels  68.6 us (99%)
    pallas_call x1, Pallas kernels, per_device(): pl.pallas_call(kernel, out_shape=shapes, in_specs=[any_spec] * 5, out_spe...  64.4 us
    pallas_call x1, Pallas kernels, per_device(): pl.pallas_call(finish, out_shape=shapes, in_specs=[any_spec] * 3, out_spe...  4.13 us

profile of v2, /device:TPU:1, one launch (start us, length us, event | category | flops | bytes accessed | tf_op | source)
XLA Modules:
  0.0 69.2 jit_solution(9601606952566381659)
XLA Ops:
  0.6 64.4 %ffn_backward.1 = (bf16[24,1536]{1,0:T(8,128)(2,1)}, bf16[1536,768]{1,0:T(8,128)(2,1)}, bf16[768,1536]{1,0:T(8,128)(2,1)}) custom-call(bf16[768,1536]{1,0:T(8,128)(2,1)} %inp_h.1, bf16[768,1536]{1,0:T(8,128)(2,1)} %og_h.1, bf16[96,768]{1,0:T(8,128)(2,1)} %pa_h.1, bf16[1536,768]{1,0:T(8,128)(2,1)} %win_h.1, bf16[768,1536]{1,0:T(8,128)(2,1)} %wout_h.1), custom_call_target="tpu_custom_call" | custom-call | tf_op jit(solution)/shard_map/ffn_backward/pallas_call | solution.py:428
  65.1 4.1 %finish.1 = (bf16[24,1536]{1,0:T(8,128)(2,1)}, bf16[1536,768]{1,0:T(8,128)(2,1)}, bf16[768,1536]{1,0:T(8,128)(2,1)}) custom-call(bf16[24,1536]{1,0:T(8,128)(2,1)} %get-tuple-element.6.gi_t, bf16[1536,768]{1,0:T(8,128)(2,1)} %get-tuple-element.7.gwi_t, bf16[768,1536]{1,0:T(8,128)(2,1)} %get-tuple-element.8.gwo_t), custom_call_target="tpu_custom_call" | custom-call | tf_op jit(solution)/shard_map/finish/pallas_call | solution.py:452
